TPU v7x, 512 devices: a whole 4x8x8 slice. The times are simulated.
512 devices in a mesh: tok: 64 (over z, y), tp: 8 (over x, core).
Axes of the slice: x: 4, y: 8, z: 8, core: 2. Of those that a mesh axis runs over, the one named last changes fastest.
Arguments:
- activations: bfloat16 [8192, 4096], P('tok', 'tp'), may hold values from -6 to 6
- out_grad: bfloat16 [8192, 4096], P('tok', 'tp'), may hold values from -6 to 6
- routes: int32 [8192, 2], P('tok'), may hold values from 0 to 63, all different within a row; in each aligned block of 128 rows (0 to 127, 128 to 255, ...) at most 8 rows name the same one
- gate_vals: float32 [8192, 2], P('tok'), may hold values from 0.2 to 1
- w_gate: bfloat16 [64, 1536, 4096], P('tok', 'tp'), may hold values from -0.09375 to 0.09375
- w_up: bfloat16 [64, 1536, 4096], P('tok', 'tp'), may hold values from -0.09375 to 0.09375
- w_down: bfloat16 [64, 1536, 4096], P('tok', 'tp'), may hold values from -0.15625 to 0.15625
Outputs:
- in_grad: bfloat16 [8192, 4096], P('tok', 'tp')
Inputs may be any that keep to these rules, and one draw needn't show every extreme that they name: `routes`: each row names 2 different experts. In each aligned block of 128 rows (the tokens of one index of tok) no expert is named by more than 8 rows, a bound that some block reaches.
All inputs are finite; a program needn't handle non-finite values.
Results may differ from a plain program's by a relative error of at most 0.0057.
Values may be sent and summed in bfloat16 or wider, within the bound.
No kernel may reach another device: no remote copies, remote signals or barrier semaphores. Data moves between devices by JAX's collectives and lax.ppermute only.
A program may use at most 64 MiB of HBM per device.

v0:
```python
import jax
import jax.numpy as jnp
from jax import lax
from jax.sharding import PartitionSpec as P


def routing(routes, n_tok, capacity):
    tok_dev = routes.shape[0]
    top_k = routes.shape[1]
    flat = routes.reshape(-1)
    onehot = (flat[:, None] == jnp.arange(n_tok, dtype=jnp.int32)[None, :]).astype(jnp.int32)
    before = jnp.cumsum(onehot, axis=0) - onehot
    slot = jnp.sum(before * onehot, axis=1)
    position = flat * capacity + slot
    slot_count = n_tok * capacity
    hits = (position[:, None] == jnp.arange(slot_count, dtype=jnp.int32)[None, :]).astype(jnp.int32)
    hits = jnp.sum(hits.reshape(tok_dev, top_k, slot_count), axis=1)
    token_of = jnp.sum(hits * jnp.arange(tok_dev, dtype=jnp.int32)[:, None], axis=0)
    filled = jnp.sum(hits, axis=0) > 0
    return (position, token_of, filled)


def bucket(rows, token_of, filled):
    return jnp.where(filled[:, None], jnp.take(rows, token_of, axis=0), jnp.zeros((), rows.dtype))


def combine(returned, position, gate_vals):
    picked = jnp.take(returned, position, axis=0).reshape(
        gate_vals.shape[0], gate_vals.shape[1], returned.shape[1]
    )
    total = jnp.zeros((picked.shape[0], picked.shape[2]), jnp.float32)
    for column in range(gate_vals.shape[1]):
        total = total + gate_vals[:, column : column + 1] * picked[:, column].astype(jnp.float32)
    return total


def hidden_grads(gate_pre, up_pre, hidden_grad):
    sigma = jax.nn.sigmoid(gate_pre)
    silu_value = gate_pre * sigma
    slope = sigma * (1.0 + gate_pre * (1.0 - sigma))
    return (
        (hidden_grad * up_pre * slope).astype(jnp.bfloat16),
        (hidden_grad * silu_value).astype(jnp.bfloat16),
    )


def shards(activations, out_grad, routes, gate_vals, w_gate, w_up, w_down):
    n_tok = lax.axis_size("tok")
    tok_dev = routes.shape[0]
    top_k = routes.shape[1]
    capacity = max(2, 2 * tok_dev * top_k // n_tok)
    slot_count = n_tok * capacity
    gate_local = w_gate[0]
    up_local = w_up[0]
    down_local = w_down[0]
    contract_last = (((1,), (1,)), ((), ()))
    position, token_of, filled = routing(routes, n_tok, capacity)
    whole_x, whole_g = (
        lax.all_gather(activations, "tp", axis=1, tiled=True),
        lax.all_gather(out_grad, "tp", axis=1, tiled=True),
    )
    width = whole_x.shape[1]
    send_x = bucket(whole_x, token_of, filled).reshape(n_tok, capacity, width)
    send_g = bucket(whole_g, token_of, filled).reshape(n_tok, capacity, width)
    recv_x, recv_g = (
        lax.all_to_all(send_x, "tok", split_axis=0, concat_axis=0, tiled=True),
        lax.all_to_all(send_g, "tok", split_axis=0, concat_axis=0, tiled=True),
    )
    recv_x = recv_x.reshape(slot_count, width)
    recv_g = recv_g.reshape(slot_count, width)
    gate_pre = lax.dot_general(
        recv_x, gate_local, contract_last, preferred_element_type=jnp.float32
    )
    up_pre = lax.dot_general(recv_x, up_local, contract_last, preferred_element_type=jnp.float32)
    hidden_grad = lax.dot_general(
        recv_g, down_local, contract_last, preferred_element_type=jnp.float32
    )
    gate_grad, up_grad = hidden_grads(gate_pre, up_pre, hidden_grad)
    partial_value = jnp.dot(gate_grad, gate_local, preferred_element_type=jnp.float32)
    partial_value = partial_value + jnp.dot(up_grad, up_local, preferred_element_type=jnp.float32)
    partial_bf = partial_value.astype(jnp.bfloat16)
    full_width = partial_bf.shape[1]
    returned = lax.all_to_all(
        partial_bf.reshape(n_tok, capacity, full_width),
        "tok",
        split_axis=0,
        concat_axis=0,
        tiled=True,
    )
    combined = combine(returned.reshape(slot_count, full_width), position, gate_vals)
    summed = lax.psum_scatter(combined, "tp", scatter_dimension=1, tiled=True)
    return summed.astype(jnp.bfloat16)


def solution(mesh):
    placed = (
        P("tok", "tp"),
        P("tok", "tp"),
        P("tok", None),
        P("tok", None),
        P("tok", "tp", None),
        P("tok", "tp", None),
        P("tok", "tp", None),
    )
    return jax.shard_map(
        shards, mesh=mesh, in_specs=placed, out_specs=P("tok", "tp"), check_vma=False
    )
```

profile of v0, /device:TPU:16, one launch (start us, length us, event | category | flops | bytes accessed | tf_op | source)
XLA Modules:
  0.0 566.2 jit_solution(14401200045992333486)
XLA Ops:
  6.5 0.0 copy-start
  6.5 0.0 all-gather.3.cloned.1.call-start
  6.5 0.7 all-gather.3.cloned.1.call-update
  7.3 0.0 all-gather.5.cloned.1.call-start
  7.3 0.7 all-gather.5.cloned.1.call-update
  8.0 0.8 copy.23
  8.8 0.1 eq.40
  8.9 0.1 reshape.106
  9.1 0.6 reduce-window.6
  9.7 0.2 slice_reduce_fusion
  9.9 0.1 fusion.43
  10.0 0.1 reduce_sum.41
  10.2 0.1 copy.26
  10.3 0.7 compare_and_fusion.1
  11.0 0.1 convert_reduce_fusion.1
  11.2 31.5 %all-gather.3.cloned.1.call-done = bf16[128,4096]{1,0:T(8,128)(2,1)} async-done(((bf16[128,512]{1,0:T(8,128)(2,1)}), bf16[128,4096]{1,0:T(8,128)(2,1)}) %all-gather.3.cloned.1.call-update) | async-done | bytes 1048592 | tf_op jit(solution)/shard_map/all_gather | solution.py:60
  42.7 9.9 %gather_fusion.1 = bf16[512,4096]{1,0:T(8,128)(2,1)} fusion(bf16[128,4096]{1,0:T(8,128)(2,1)} %all-gather.3.cloned.1.call-done, s32[1024]{0:T(1024)S(1)} %pad_clamp_fusion.1), kind=kCustom, calls=%fused_computation.clone | custom fusion | bytes 8390656 | tf_op jit(solution)/shard_map/jit(_take)/gather | solution.py:24
  52.6 20.9 %all-gather.5.cloned.1.call-done = bf16[128,4096]{1,0:T(8,128)(2,1)} async-done(((bf16[128,512]{1,0:T(8,128)(2,1)}), bf16[128,4096]{1,0:T(8,128)(2,1)}) %all-gather.5.cloned.1.call-update) | async-done | bytes 1048592 | tf_op jit(solution)/shard_map/all_gather | solution.py:59
  73.5 9.9 %gather_fusion.2 = bf16[512,4096]{1,0:T(8,128)(2,1)} fusion(bf16[128,4096]{1,0:T(8,128)(2,1)} %all-gather.5.cloned.1.call-done, s32[1024]{0:T(1024)S(1)} %pad_clamp_fusion.1), kind=kCustom, calls=%fused_computation.1.clone | custom fusion | bytes 8390656 | tf_op jit(solution)/shard_map/jit(_take)/gather | solution.py:24
  83.4 5.4 fusion.7
  88.8 109.8 %all_to_all.15 = bf16[64,8,4096]{2,1,0:T(8,128)(2,1)} all-to-all(bf16[64,8,4096]{2,1,0:T(8,128)(2,1)S(1)} %get-tuple-element.12), channel_id=1, replica_groups=mesh['tok'=64,'tp'=8] {'tok'}, dimensions={0} | all-to-all | bytes 8388608 | tf_op jit(solution)/shard_map/all_to_all | solution.py:66
  198.5 0.0 copy-start.1
  198.5 16.3 %all-to-all-start = ((bf16[64,8,4096]{2,1,0:T(8,128)(2,1)}), bf16[64,8,4096]{2,1,0:T(8,128)(2,1)}, u32[]{:S(2)}, u32[]{:S(2)}) async-start(bf16[64,8,4096]{2,1,0:T(8,128)(2,1)} %get-tuple-element.13), calls=%async_computation | async-start | bytes 8388608 | tf_op jit(solution)/shard_map/all_to_all | solution.py:67
  214.9 0.0 copy-done.1
  214.9 3.7 fusion.1
  218.6 114.2 %all-to-all-done = bf16[64,8,4096]{2,1,0:T(8,128)(2,1)} async-done(((bf16[64,8,4096]{2,1,0:T(8,128)(2,1)}), bf16[64,8,4096]{2,1,0:T(8,128)(2,1)}, u32[]{:S(2)}, u32[]{:S(2)}) %all-to-all-start) | async-done | bytes 4194336 | tf_op jit(solution)/shard_map/all_to_all | solution.py:67
  332.8 5.0 fusion.5
  337.8 0.0 copy-done
  337.8 8.3 %fusion.10 = f32[512,4096]{1,0:T(8,128)} fusion(bf16[1,192,4096]{2,1,0:T(8,128)(2,1)S(1)} %copy-done.1, f32[512,192]{0,1:T(8,128)} %fusion.5, bf16[1,192,4096]{2,1,0:T(8,128)(2,1)S(1)} %copy-done, bf16[64,8,4096]{2,1,0:T(8,128)(2,1)} %all_to_all.15, f32[512,192]{0,1:T(8,128)S(1)} %fusion.1), kind=kOutput, calls=%fused_computation.19 | convolution fusion | flops 1611595776 | bytes 16515072 | tf_op jit(solution)/shard_map/dot_general | solution.py:79
  346.1 6.8 %fusion = bf16[64,8,4096]{2,1,0:T(8,128)(2,1)} fusion(f32[512,4096]{1,0:T(8,128)} %fusion.10, bf16[1,192,4096]{2,1,0:T(8,128)(2,1)S(1)} %copy-done, f32[512,192]{0,1:T(8,128)} %fusion.5, f32[512,192]{0,1:T(8,128)S(1)} %fusion.1), kind=kOutput, calls=%fused_computation.4 | convolution fusion | flops 810090496 | bytes 14942208 | tf_op jit(solution)/shard_map/dot_general | solution.py:80
  353.0 0.0 copy-start.2
  353.0 0.0 copy-start.3
  353.0 15.8 %all-to-all-start.2 = ((bf16[64,8,4096]{2,1,0:T(8,128)(2,1)}), bf16[64,8,4096]{2,1,0:T(8,128)(2,1)}, u32[]{:S(2)}, u32[]{:S(2)}) async-start(bf16[64,8,4096]{2,1,0:T(8,128)(2,1)} %fusion), calls=%async_computation.2 | async-start | bytes 8388608 | tf_op jit(solution)/shard_map/all_to_all | solution.py:83
  368.8 0.3 reduce-scatter.2.cloned.1.call-start
  369.1 0.0 copy-done.2
  369.1 0.1 copy.27
  369.2 0.1 mul.84
  369.4 0.0 copy-done.3
  369.4 110.9 %all-to-all-done.2 = bf16[64,8,4096]{2,1,0:T(8,128)(2,1)} async-done(((bf16[64,8,4096]{2,1,0:T(8,128)(2,1)}), bf16[64,8,4096]{2,1,0:T(8,128)(2,1)}, u32[]{:S(2)}, u32[]{:S(2)}) %all-to-all-start.2) | async-done | bytes 4194336 | tf_op jit(solution)/shard_map/all_to_all | solution.py:83
  480.3 7.9 %gather_fusion = bf16[256,4096]{1,0:T(8,128)(2,1)} fusion(bf16[512,4096]{1,0:T(8,128)(2,1)} %bitcast.10, s32[1024]{0:T(1024)S(1)} %pad_clamp_fusion), kind=kCustom, calls=%fused_computation.2 | custom fusion | bytes 4195328 | tf_op jit(solution)/shard_map/jit(_take)/gather | solution.py:28
  488.3 4.4 gather.10
  492.7 4.0 copy_select_fusion
  496.7 1.8 fusion.9
  498.5 0.0 reduce-scatter.2.cloned.1.call-update
  498.5 59.6 %reduce-scatter.2.cloned.1.call-done = f32[128,512]{1,0:T(8,128)} async-done(((f32[128,4096]{1,0:T(8,128)}), f32[128,512]{1,0:T(8,128)}) %reduce-scatter.2.cloned.1.call-update) | async-done | bytes 262160 | tf_op jit(solution)/shard_map/reduce_scatter | solution.py:91
  558.1 1.6 convert_element_type.45
  (11 shorter events, 0.1 us)
Async XLA Ops:
  6.5 331.3 %copy-start = (bf16[1,192,4096]{2,1,0:T(8,128)(2,1)S(1)}, bf16[1,192,4096]{2,1,0:T(8,128)(2,1)}, u32[]{:S(2)}) copy-start(bf16[1,192,4096]{2,1,0:T(8,128)(2,1)} %param.14) | copy-start | bytes 4718596
  6.5 36.1 %all-gather.3.cloned.1.call-start = ((), (), s32[]{:S(2)}) async-start(), calls=%async_computation.4 | async-start | bytes 1179648 | tf_op jit(solution)/shard_map/all_gather | solution.py:60
  7.3 66.2 %all-gather.5.cloned.1.call-start = ((), (), s32[]{:S(2)}) async-start(), calls=%async_computation.5 | async-start | bytes 1179648 | tf_op jit(solution)/shard_map/all_gather | solution.py:59
  198.5 16.4 %copy-start.1 = (bf16[1,192,4096]{2,1,0:T(8,128)(2,1)S(1)}, bf16[1,192,4096]{2,1,0:T(8,128)(2,1)}, u32[]{:S(2)}) copy-start(bf16[1,192,4096]{2,1,0:T(8,128)(2,1)} %param.13) | copy-start | bytes 4718596
  198.5 134.3 %all-to-all-start = ((bf16[64,8,4096]{2,1,0:T(8,128)(2,1)}), bf16[64,8,4096]{2,1,0:T(8,128)(2,1)}, u32[]{:S(2)}, u32[]{:S(2)}) async-start(bf16[64,8,4096]{2,1,0:T(8,128)(2,1)} %get-tuple-element.13), calls=%async_computation | async-start | bytes 8388608 | tf_op jit(solution)/shard_map/all_to_all | solution.py:67
  353.0 16.1 %copy-start.2 = (s32[128,2]{0,1:T(2,128)S(1)}, s32[128,2]{0,1:T(2,128)}, u32[]{:S(2)}) copy-start(s32[128,2]{0,1:T(2,128)} %param.11) | copy-start | bytes 3076
  353.0 16.4 %copy-start.3 = (f32[128,2]{0,1:T(2,128)S(1)}, f32[128,2]{0,1:T(2,128)}, u32[]{:S(2)}) copy-start(f32[128,2]{0,1:T(2,128)} %param.12) | copy-start | bytes 3076
  353.0 127.4 %all-to-all-start.2 = ((bf16[64,8,4096]{2,1,0:T(8,128)(2,1)}), bf16[64,8,4096]{2,1,0:T(8,128)(2,1)}, u32[]{:S(2)}, u32[]{:S(2)}) async-start(bf16[64,8,4096]{2,1,0:T(8,128)(2,1)} %fusion), calls=%async_computation.2 | async-start | bytes 8388608 | tf_op jit(solution)/shard_map/all_to_all | solution.py:83
  368.8 189.3 %reduce-scatter.2.cloned.1.call-start = ((), (), s32[]{:S(2)}) async-start(), calls=%async_computation.6 | async-start | bytes 2359296 | tf_op jit(solution)/shard_map/reduce_scatter | solution.py:91
Sparse Core Ops, SparseCore 0:
  9.5 33.1 all-gather.2
  44.8 28.5 all-gather.4
  498.6 59.3 reduce-scatter.1
where the time goes:
time: 567 us; the launch traced here: 566 us
  waiting for transfers between devices  338 us (60%)
  blocking collectives  110 us (19%)
  local copies, waits for them, and re-layouts  33.9 us (6%)
  starting transfers between devices  32.5 us (6%)
  matrix products  23.8 us (4%)
  other arithmetic  14.5 us (3%)
  between operations  13.2 us (2%)
    all_to_all x1, waiting for transfers between devices, shards(): lax.all_to_all(send_g, 'tok', split_axis=0, concat_axis=0, tiled=True)  114 us
    all_to_all x1, waiting for transfers between devices, shards(): lax.all_to_all(partial_bf.reshape(n_tok, capacity, full_width), 'tok', sp...  111 us
    all_to_all x1, blocking collectives, shards(): lax.all_to_all(send_x, 'tok', split_axis=0, concat_axis=0, tiled=True)  110 us
    reduce_scatter x1, waiting for transfers between devices, shards(): summed = lax.psum_scatter(combined, 'tp', scatter_dimension=1, tiled=True)  59.6 us
    all_gather x1, waiting for transfers between devices, shards(): lax.all_gather(out_grad, 'tp', axis=1, tiled=True)  31.5 us
    all_gather x1, waiting for transfers between devices, shards(): lax.all_gather(activations, 'tp', axis=1, tiled=True)  20.9 us
    gather x2, local copies, waits for them, and re-layouts, bucket(): jnp.take(rows, token_of, axis=0)  19.8 us
    all_to_all x1, starting transfers between devices, shards(): lax.all_to_all(send_g, 'tok', split_axis=0, concat_axis=0, tiled=True)  16.3 us
  transfers between devices with their start and end apart: 5, of which 5 were waited for; matrix products, arithmetic and copies ran while one was open for 3% of the time, Pallas kernels for 0%

commit v1 on v0

--- a/solution.py
+++ b/solution.py
@@ -56,7 +56,9 @@
     contract_last = (((1,), (1,)), ((), ()))
     position, token_of, filled = routing(routes, n_tok, capacity)
     whole_x, whole_g = (
-        lax.all_gather(activations, "tp", axis=1, tiled=True),
+        jnp.concatenate(
+            lax.all_to_all(jnp.stack([activations] * lax.axis_size("tp")), "tp", 0, 0), axis=1
+        ),
         lax.all_gather(out_grad, "tp", axis=1, tiled=True),
     )
     width = whole_x.shape[1]

time: 567 us -> 536 us (0.945)
  the two profiles are of different devices: /device:TPU:16 before, /device:TPU:8 now
where the time goes in v1:
time: 536 us; the launch traced here: 535 us
  waiting for transfers between devices  305 us (57%)
  blocking collectives  111 us (21%)
  starting transfers between devices  36 us (7%)
  local copies, waits for them, and re-layouts  32.1 us (6%)
  matrix products  23.8 us (4%)
  other arithmetic  13.8 us (3%)
  between operations  13.5 us (3%)
    all_to_all x1, waiting for transfers between devices, shards(): lax.all_to_all(send_g, 'tok', split_axis=0, concat_axis=0, tiled=True)  114 us
    all_to_all x1, waiting for transfers between devices, shards(): lax.all_to_all(partial_bf.reshape(n_tok, capacity, full_width), 'tok', sp...  113 us
    all_to_all x1, blocking collectives, shards(): lax.all_to_all(send_x, 'tok', split_axis=0, concat_axis=0, tiled=True)  111 us
    reduce_scatter x1, waiting for transfers between devices, shards(): summed = lax.psum_scatter(combined, 'tp', scatter_dimension=1, tiled=True)  56.7 us
    all_to_all x1, starting transfers between devices, shards(): lax.all_to_all(partial_bf.reshape(n_tok, capacity, full_width), 'tok', sp...  16.1 us
    all_to_all x1, starting transfers between devices, shards(): lax.all_to_all(send_g, 'tok', split_axis=0, concat_axis=0, tiled=True)  15.3 us
    gather x2, local copies, waits for them, and re-layouts, bucket(): jnp.take(rows, token_of, axis=0)  14.3 us
    all_to_all x1, waiting for transfers between devices, shards(): lax.all_to_all(jnp.stack([activations] * lax.axis_size('tp')), 'tp', 0, 0)  14.1 us
  transfers between devices with their start and end apart: 5, of which 5 were waited for; matrix products, arithmetic and copies ran while one was open for 3% of the time, Pallas kernels for 0%

profile of v1, /device:TPU:8, one launch (start us, length us, event | category | flops | bytes accessed | tf_op | source)
XLA Modules:
  0.0 535.4 jit_solution(11491883764416016530)
XLA Ops:
  6.5 0.0 copy-start
  6.5 0.0 copy-start.3
  6.5 0.0 all-gather.2.cloned.1.call-start
  6.5 0.7 all-gather.2.cloned.1.call-update
  7.3 2.0 stack.2
  9.3 4.3 all-to-all-start.1
  13.6 0.0 copy-done.3
  13.6 0.1 copy.31
  13.7 0.1 eq.40
  13.8 0.1 reshape.114
  14.0 0.6 reduce-window.6
  14.6 0.2 slice_reduce_fusion
  14.8 0.1 fusion.43
  15.0 0.1 reduce_sum.41
  15.1 0.1 copy.34
  15.2 0.1 convert_reduce_fusion.1
  15.4 14.1 %all-to-all-done.1 = bf16[8,128,512]{2,1,0:T(8,128)(2,1)S(1)} async-done(((bf16[8,128,512]{2,1,0:T(8,128)(2,1)}), bf16[8,128,512]{2,1,0:T(8,128)(2,1)S(1)}, u32[]{:S(2)}, u32[]{:S(2)}) %all-to-all-start.1) | async-done | bytes 1048608 | tf_op jit(solution)/shard_map/all_to_all | solution.py:60
  29.6 0.0 copy-start.1
  29.6 1.0 copy-done.1
  30.6 1.3 copy.39
  31.9 4.4 gather_fusion.2
  36.3 6.4 %all-gather.2.cloned.1.call-done = bf16[128,4096]{1,0:T(8,128)(2,1)} async-done(((bf16[128,512]{1,0:T(8,128)(2,1)}), bf16[128,4096]{1,0:T(8,128)(2,1)}) %all-gather.2.cloned.1.call-update) | async-done | bytes 1048592 | tf_op jit(solution)/shard_map/all_gather | solution.py:62
  42.8 9.9 %gather_fusion.1 = bf16[512,4096]{1,0:T(8,128)(2,1)} fusion(bf16[128,4096]{1,0:T(8,128)(2,1)} %all-gather.2.cloned.1.call-done, s32[1024]{0:T(1024)S(1)} %pad_clamp_fusion.1), kind=kCustom, calls=%fused_computation.clone | custom fusion | bytes 8390656 | tf_op jit(solution)/shard_map/jit(_take)/gather | solution.py:24
  52.7 5.3 fusion.7
  58.0 110.9 %all_to_all.20 = bf16[64,8,4096]{2,1,0:T(8,128)(2,1)} all-to-all(bf16[64,8,4096]{2,1,0:T(8,128)(2,1)S(1)} %get-tuple-element.12), channel_id=1, replica_groups=mesh['tok'=64,'tp'=8] {'tok'}, dimensions={0} | all-to-all | bytes 8388608 | tf_op jit(solution)/shard_map/all_to_all | solution.py:68
  168.9 0.0 copy-start.2
  168.9 15.3 %all-to-all-start = ((bf16[64,8,4096]{2,1,0:T(8,128)(2,1)}), bf16[64,8,4096]{2,1,0:T(8,128)(2,1)}, u32[]{:S(2)}, u32[]{:S(2)}) async-start(bf16[64,8,4096]{2,1,0:T(8,128)(2,1)} %get-tuple-element.13), calls=%async_computation | async-start | bytes 8388608 | tf_op jit(solution)/shard_map/all_to_all | solution.py:69
  184.2 0.0 copy-done.2
  184.2 3.7 fusion.1
  187.9 114.0 %all-to-all-done = bf16[64,8,4096]{2,1,0:T(8,128)(2,1)} async-done(((bf16[64,8,4096]{2,1,0:T(8,128)(2,1)}), bf16[64,8,4096]{2,1,0:T(8,128)(2,1)}, u32[]{:S(2)}, u32[]{:S(2)}) %all-to-all-start) | async-done | bytes 4194336 | tf_op jit(solution)/shard_map/all_to_all | solution.py:69
  301.9 5.0 fusion.5
  306.9 0.0 copy-done
  306.9 8.3 %fusion.10 = f32[512,4096]{1,0:T(8,128)} fusion(bf16[1,192,4096]{2,1,0:T(8,128)(2,1)S(1)} %copy-done.2, f32[512,192]{0,1:T(8,128)} %fusion.5, bf16[1,192,4096]{2,1,0:T(8,128)(2,1)S(1)} %copy-done, bf16[64,8,4096]{2,1,0:T(8,128)(2,1)} %all_to_all.20, f32[512,192]{0,1:T(8,128)S(1)} %fusion.1), kind=kOutput, calls=%fused_computation.19 | convolution fusion | flops 1611595776 | bytes 16515072 | tf_op jit(solution)/shard_map/dot_general | solution.py:81
  315.2 6.8 %fusion = bf16[64,8,4096]{2,1,0:T(8,128)(2,1)} fusion(f32[512,4096]{1,0:T(8,128)} %fusion.10, bf16[1,192,4096]{2,1,0:T(8,128)(2,1)S(1)} %copy-done, f32[512,192]{0,1:T(8,128)} %fusion.5, f32[512,192]{0,1:T(8,128)S(1)} %fusion.1), kind=kOutput, calls=%fused_computation.4 | convolution fusion | flops 810090496 | bytes 14942208 | tf_op jit(solution)/shard_map/dot_general | solution.py:82
  322.0 0.0 copy-start.4
  322.0 16.1 %all-to-all-start.3 = ((bf16[64,8,4096]{2,1,0:T(8,128)(2,1)}), bf16[64,8,4096]{2,1,0:T(8,128)(2,1)}, u32[]{:S(2)}, u32[]{:S(2)}) async-start(bf16[64,8,4096]{2,1,0:T(8,128)(2,1)} %fusion), calls=%async_computation.3 | async-start | bytes 8388608 | tf_op jit(solution)/shard_map/all_to_all | solution.py:85
  338.1 0.3 reduce-scatter.2.cloned.1.call-start
  338.4 0.1 copy.36
  338.5 0.1 mul.84
  338.7 0.0 copy-done.4
  338.7 113.3 %all-to-all-done.3 = bf16[64,8,4096]{2,1,0:T(8,128)(2,1)} async-done(((bf16[64,8,4096]{2,1,0:T(8,128)(2,1)}), bf16[64,8,4096]{2,1,0:T(8,128)(2,1)}, u32[]{:S(2)}, u32[]{:S(2)}) %all-to-all-start.3) | async-done | bytes 4194336 | tf_op jit(solution)/shard_map/all_to_all | solution.py:85
  452.0 7.9 %gather_fusion = bf16[256,4096]{1,0:T(8,128)(2,1)} fusion(bf16[512,4096]{1,0:T(8,128)(2,1)} %bitcast.11, s32[1024]{0:T(1024)S(1)} %pad_clamp_fusion), kind=kCustom, calls=%fused_computation.2 | custom fusion | bytes 4195328 | tf_op jit(solution)/shard_map/jit(_take)/gather | solution.py:28
  460.0 4.4 gather.10
  464.4 4.0 copy_select_fusion
  468.4 1.8 fusion.9
  470.2 0.0 reduce-scatter.2.cloned.1.call-update
  470.2 56.7 %reduce-scatter.2.cloned.1.call-done = f32[128,512]{1,0:T(8,128)} async-done(((f32[128,4096]{1,0:T(8,128)}), f32[128,512]{1,0:T(8,128)}) %reduce-scatter.2.cloned.1.call-update) | async-done | bytes 262160 | tf_op jit(solution)/shard_map/reduce_scatter | solution.py:93
  526.9 1.6 convert_element_type.45
  (12 shorter events, 0.2 us)
Async XLA Ops:
  6.5 300.3 %copy-start = (bf16[1,192,4096]{2,1,0:T(8,128)(2,1)S(1)}, bf16[1,192,4096]{2,1,0:T(8,128)(2,1)}, u32[]{:S(2)}) copy-start(bf16[1,192,4096]{2,1,0:T(8,128)(2,1)} %param.14) | copy-start | bytes 4718596
  6.5 7.1 %copy-start.3 = (s32[128,2]{0,1:T(2,128)S(1)}, s32[128,2]{0,1:T(2,128)}, u32[]{:S(2)}) copy-start(s32[128,2]{0,1:T(2,128)} %param.11) | copy-start | bytes 3076
  6.5 36.2 %all-gather.2.cloned.1.call-start = ((), (), s32[]{:S(2)}) async-start(), calls=%async_computation.5 | async-start | bytes 1179648 | tf_op jit(solution)/shard_map/all_gather | solution.py:62
  9.3 20.3 %all-to-all-start.1 = ((bf16[8,128,512]{2,1,0:T(8,128)(2,1)}), bf16[8,128,512]{2,1,0:T(8,128)(2,1)S(1)}, u32[]{:S(2)}, u32[]{:S(2)}) async-start(bf16[8,128,512]{2,1,0:T(8,128)(2,1)} %stack.2), calls=%async_computation.1 | async-start | bytes 2097152 | tf_op jit(solution)/shard_map/all_to_all | solution.py:60
  29.6 1.0 copy-start.1
  168.9 15.3 %copy-start.2 = (bf16[1,192,4096]{2,1,0:T(8,128)(2,1)S(1)}, bf16[1,192,4096]{2,1,0:T(8,128)(2,1)}, u32[]{:S(2)}) copy-start(bf16[1,192,4096]{2,1,0:T(8,128)(2,1)} %param.13) | copy-start | bytes 4718596
  168.9 133.0 %all-to-all-start = ((bf16[64,8,4096]{2,1,0:T(8,128)(2,1)}), bf16[64,8,4096]{2,1,0:T(8,128)(2,1)}, u32[]{:S(2)}, u32[]{:S(2)}) async-start(bf16[64,8,4096]{2,1,0:T(8,128)(2,1)} %get-tuple-element.13), calls=%async_computation | async-start | bytes 8388608 | tf_op jit(solution)/shard_map/all_to_all | solution.py:69
  322.0 16.7 %copy-start.4 = (f32[128,2]{0,1:T(2,128)S(1)}, f32[128,2]{0,1:T(2,128)}, u32[]{:S(2)}) copy-start(f32[128,2]{0,1:T(2,128)} %param.12) | copy-start | bytes 3076
  322.0 130.0 %all-to-all-start.3 = ((bf16[64,8,4096]{2,1,0:T(8,128)(2,1)}), bf16[64,8,4096]{2,1,0:T(8,128)(2,1)}, u32[]{:S(2)}, u32[]{:S(2)}) async-start(bf16[64,8,4096]{2,1,0:T(8,128)(2,1)} %fusion), calls=%async_computation.3 | async-start | bytes 8388608 | tf_op jit(solution)/shard_map/all_to_all | solution.py:85
  338.1 188.8 %reduce-scatter.2.cloned.1.call-start = ((), (), s32[]{:S(2)}) async-start(), calls=%async_computation.6 | async-start | bytes 2359296 | tf_op jit(solution)/shard_map/reduce_scatter | solution.py:93
Sparse Core Ops, SparseCore 0:
  9.5 33.2 all-gather.1
  470.3 56.5 reduce-scatter.1
